TPU v7x, 128 devices: a whole 4x4x4 slice. The times are simulated.
128 devices in a mesh: row: 8 (over z, core), col: 16 (over y, x).
Axes of the slice: x: 4, y: 4, z: 4, core: 2. Of those that a mesh axis runs over, the one named last changes fastest.
Arguments:
- symmetric: float32 [16384, 16384], P('row', 'col'), may hold values from -8 to 8, as said below
- reflectors: float32 [4, 64, 16384], P(None, None, ('row', 'col')), may hold values from -0.125 to 0.125
- tri_factor: float32 [4, 64, 64], replicated, may hold values from -0.4 to 1.5, as said below
Outputs:
- updated: float32 [16384, 16384], P('row', 'col')
Inputs may be any that keep to these rules, and one draw needn't show every extreme that they name: symmetric is a symmetric matrix. Each tri_factor[p] is upper triangular.
All inputs are finite; a program needn't handle non-finite values.
Results may differ from a plain program's by a relative error of at most 0.00029.
Values sent between devices are 32-bit elements; how exact they have to be, the bound alone decides.
A program may use at most 64 MiB of HBM per device.

v0:
```python
import jax
import jax.numpy as jnp
from jax import lax
from jax.sharding import PartitionSpec as P


def broadcast(value, axis, source):
    kept = jnp.where(lax.axis_index(axis) == source, value, 0).astype(value.dtype)
    return lax.psum(kept, axis)


def shards(symmetric, reflectors, tri_factor):
    highest = lax.Precision.HIGHEST
    cols_here = symmetric.shape[1]
    row_count = lax.axis_size("row")
    col_count = lax.axis_size("col")
    col_index = lax.axis_index("col")
    owner = col_index * row_count // col_count
    offset = col_index % (col_count // row_count) * cols_here
    matrix = symmetric
    for panel in range(reflectors.shape[0]):
        piece = reflectors[panel]
        factor = tri_factor[panel]
        reflect_rows = lax.all_gather(piece, "col", axis=1, tiled=True)
        reflect_cols = broadcast(
            lax.dynamic_slice_in_dim(reflect_rows, offset, cols_here, 1), "row", owner
        )
        partial_value = lax.dot_general(
            reflect_cols,
            matrix,
            (((1,), (1,)), ((), ())),
            precision=highest,
            preferred_element_type=jnp.float32,
        )
        product_rows = lax.psum(partial_value, "col")
        image_rows = jnp.dot(
            factor.T, product_rows, precision=highest, preferred_element_type=jnp.float32
        )
        local_inner = lax.dot_general(
            reflect_rows,
            image_rows,
            (((1,), (1,)), ((), ())),
            precision=highest,
            preferred_element_type=jnp.float32,
        )
        inner = lax.psum(local_inner, "row")
        coupling = jnp.dot(factor.T, inner, precision=highest, preferred_element_type=jnp.float32)
        update_rows = image_rows - 0.5 * jnp.dot(
            coupling.T, reflect_rows, precision=highest, preferred_element_type=jnp.float32
        )
        update_cols = broadcast(
            lax.dynamic_slice_in_dim(update_rows, offset, cols_here, 1), "row", owner
        )
        left_block = jnp.concatenate([reflect_rows, update_rows], axis=0)
        right_block = jnp.concatenate([update_cols, reflect_cols], axis=0)
        matrix = matrix - lax.dot_general(
            left_block,
            right_block,
            (((0,), (0,)), ((), ())),
            precision=highest,
            preferred_element_type=jnp.float32,
        )
    return matrix


def solution(mesh):
    placed = (P("row", "col"), P(None, None, ("row", "col")), P())
    return jax.shard_map(
        shards, mesh=mesh, in_specs=placed, out_specs=P("row", "col"), check_vma=False
    )
```

profile of v0, /device:TPU:0, one launch (start us, length us, event | category | flops | bytes accessed | tf_op | source)
XLA Modules:
  0.0 878.7 jit_solution(7771888216284126579)
XLA Ops:
  6.5 0.9 fusion.64
  7.4 25.2 %all-gather = f32[1,64,2048]{2,1,0:T(8,128)S(1)} all-gather(f32[1,64,128]{2,1,0:T(8,128)S(1)} %get-tuple-element.13), channel_id=2, replica_groups=mesh['row'=8,'col'=16] {'col'}, dimensions={2}, use_global_device_ids=true | all-gather | bytes 557056 | tf_op jit(solution)/shard_map/all_gather | solution.py:24
  32.6 0.7 select_bitcast_fusion.3
  33.4 60.0 %all-reduce.13.cloned.1.call-done = f32[64,1024]{1,0:T(8,128)} async-done(((f32[64,1024]{1,0:T(8,128)}), f32[64,1024]{1,0:T(8,128)}) %all-reduce.13.cloned.1.call-update) | async-done | bytes 262160 | tf_op jit(solution)/shard_map/psum | solution.py:9
  93.4 12.3 %fusion.65 = f32[64,2048]{1,0:T(8,128)} fusion(f32[64,1024]{1,0:T(8,128)} %all-reduce.13.cloned.1.call-done, f32[2048,1024]{1,0:T(8,128)} %param.3), kind=kOutput, calls=%fused_computation.85 | convolution fusion | flops 1610612736 | bytes 9175040 | tf_op jit(solution)/shard_map/dot_general | solution.py:28
  105.7 25.3 %all-gather.1 = f32[1,64,2048]{2,1,0:T(8,128)S(1)} all-gather(f32[1,64,128]{2,1,0:T(8,128)S(1)} %get-tuple-element.12), channel_id=3, replica_groups=mesh['row'=8,'col'=16] {'col'}, dimensions={2}, use_global_device_ids=true | all-gather | bytes 557056 | tf_op jit(solution)/shard_map/all_gather | solution.py:24
  131.0 0.7 select_bitcast_fusion.2
  131.7 58.1 %all-reduce.15.cloned.1.call-done = f32[64,2048]{1,0:T(8,128)} async-done(((f32[64,2048]{1,0:T(8,128)}), f32[64,2048]{1,0:T(8,128)}) %all-reduce.15.cloned.1.call-update) | async-done | bytes 524304 | tf_op jit(solution)/shard_map/psum | solution.py:35
  189.9 1.7 fusion.42
  191.5 0.6 convolution_bitcast_fusion.3
  192.1 24.4 %psum.114 = f32[64,64]{0,1:T(8,128)S(1)} all-reduce(f32[64,64]{0,1:T(8,128)S(1)} %convolution_bitcast_fusion.3), channel_id=1, replica_groups=mesh['row'=8,'col'=16] {'row'}, use_global_device_ids=true, to_apply=%region_2.3 | all-reduce | flops 4096 | bytes 32768 | tf_op jit(solution)/shard_map/psum | solution.py:46
  216.7 0.6 fusion.3
  217.3 0.7 dynamic-slice_select_fusion.3
  218.3 57.3 %all-reduce.29.cloned.1.call-done = (f32[64,1024]{1,0:T(8,128)}, f32[64,1024]{1,0:T(8,128)}) async-done(((f32[64,1024]{1,0:T(8,128)}, f32[64,1024]{1,0:T(8,128)}), (f32[64,1024]{1,0:T(8,128)}, f32[64,1024]{1,0:T(8,128)})) %all-reduce.29.cloned.1.call-update) | async-done | bytes 524304 | tf_op jit(solution)/shard_map/psum | solution.py:9
  275.6 12.9 %convolution_subtract_fusion.3 = f32[2048,1024]{1,0:T(8,128)S(1)} fusion(f32[2048,1024]{1,0:T(8,128)} %param.3, f32[64,2048]{1,0:T(8,128)S(1)} %fusion.3, f32[64,2048]{1,0:T(8,128)S(1)} %bitcast.91, f32[64,1024]{1,0:T(8,128)S(1)} %copy-done.6, f32[64,1024]{1,0:T(8,128)} %get-tuple-element.9), kind=kOutput, calls=%fused_computation.3 | convolution fusion | flops 3223715840 | bytes 18350080 | tf_op jit(solution)/shard_map/dot_general | solution.py:56
  288.5 3.4 copy-done.1
  291.9 8.9 %fusion.66 = f32[64,2048]{1,0:T(8,128)} fusion(f32[64,1024]{1,0:T(8,128)S(1)} %copy-done.4, f32[2048,1024]{1,0:T(8,128)S(1)} %convolution_subtract_fusion.3), kind=kOutput, calls=%fused_computation.86 | convolution fusion | flops 1610612736 | bytes 9175040 | tf_op jit(solution)/shard_map/dot_general | solution.py:28
  300.8 25.4 %all-gather.2 = f32[1,64,2048]{2,1,0:T(8,128)S(1)} all-gather(f32[1,64,128]{2,1,0:T(8,128)S(1)} %get-tuple-element.14), channel_id=4, replica_groups=mesh['row'=8,'col'=16] {'col'}, dimensions={2}, use_global_device_ids=true | all-gather | bytes 557056 | tf_op jit(solution)/shard_map/all_gather | solution.py:24
  326.2 0.7 select_bitcast_fusion.1
  327.0 58.3 %all-reduce.17.cloned.1.call-done = f32[64,2048]{1,0:T(8,128)} async-done(((f32[64,2048]{1,0:T(8,128)}), f32[64,2048]{1,0:T(8,128)}) %all-reduce.17.cloned.1.call-update) | async-done | bytes 524304 | tf_op jit(solution)/shard_map/psum | solution.py:35
  385.2 1.7 fusion.38
  386.9 0.6 convolution_bitcast_fusion.2
  387.5 24.4 %psum.118 = f32[64,64]{0,1:T(8,128)S(1)} all-reduce(f32[64,64]{0,1:T(8,128)S(1)} %convolution_bitcast_fusion.2), channel_id=1, replica_groups=mesh['row'=8,'col'=16] {'row'}, use_global_device_ids=true, to_apply=%region_6.7 | all-reduce | flops 4096 | bytes 32768 | tf_op jit(solution)/shard_map/psum | solution.py:46
  412.1 0.6 fusion.2
  412.6 0.7 dynamic-slice_select_fusion.2
  413.8 57.1 %all-reduce.27.cloned.1.call-done = (f32[64,1024]{1,0:T(8,128)}, f32[64,1024]{1,0:T(8,128)}) async-done(((f32[64,1024]{1,0:T(8,128)}, f32[64,1024]{1,0:T(8,128)}), (f32[64,1024]{1,0:T(8,128)}, f32[64,1024]{1,0:T(8,128)})) %all-reduce.27.cloned.1.call-update) | async-done | bytes 524304 | tf_op jit(solution)/shard_map/psum | solution.py:9
  471.0 12.9 %convolution_subtract_fusion.2 = f32[2048,1024]{1,0:T(8,128)S(1)} fusion(f32[2048,1024]{1,0:T(8,128)} %copy-done.1, f32[64,2048]{1,0:T(8,128)S(1)} %fusion.2, f32[64,2048]{1,0:T(8,128)S(1)} %bitcast.89, f32[64,1024]{1,0:T(8,128)S(1)} %copy-done.4, f32[64,1024]{1,0:T(8,128)} %get-tuple-element.7), kind=kOutput, calls=%fused_computation.2 | convolution fusion | flops 3223715840 | bytes 18350080 | tf_op jit(solution)/shard_map/dot_general | solution.py:56
  483.9 3.4 copy-done
  487.3 8.9 %fusion.67 = f32[64,2048]{1,0:T(8,128)} fusion(f32[64,1024]{1,0:T(8,128)S(1)} %copy-done.3, f32[2048,1024]{1,0:T(8,128)S(1)} %convolution_subtract_fusion.2), kind=kOutput, calls=%fused_computation.87 | convolution fusion | flops 1610612736 | bytes 9175040 | tf_op jit(solution)/shard_map/dot_general | solution.py:28
  496.2 25.4 %all-gather.3 = f32[1,64,2048]{2,1,0:T(8,128)S(1)} all-gather(f32[1,64,128]{2,1,0:T(8,128)S(1)} %get-tuple-element.11), channel_id=5, replica_groups=mesh['row'=8,'col'=16] {'col'}, dimensions={2}, use_global_device_ids=true | all-gather | bytes 557056 | tf_op jit(solution)/shard_map/all_gather | solution.py:24
  521.6 0.7 select_bitcast_fusion
  522.4 58.3 %all-reduce.19.cloned.1.call-done = f32[64,2048]{1,0:T(8,128)} async-done(((f32[64,2048]{1,0:T(8,128)}), f32[64,2048]{1,0:T(8,128)}) %all-reduce.19.cloned.1.call-update) | async-done | bytes 524304 | tf_op jit(solution)/shard_map/psum | solution.py:35
  580.6 1.7 fusion.34
  582.3 0.6 convolution_bitcast_fusion.1
  582.9 24.4 %psum.122 = f32[64,64]{0,1:T(8,128)S(1)} all-reduce(f32[64,64]{0,1:T(8,128)S(1)} %convolution_bitcast_fusion.1), channel_id=1, replica_groups=mesh['row'=8,'col'=16] {'row'}, use_global_device_ids=true, to_apply=%region_10.11 | all-reduce | flops 4096 | bytes 32768 | tf_op jit(solution)/shard_map/psum | solution.py:46
  607.5 0.6 fusion.1
  608.1 0.7 dynamic-slice_select_fusion.1
  609.0 57.3 %all-reduce.25.cloned.1.call-done = (f32[64,1024]{1,0:T(8,128)}, f32[64,1024]{1,0:T(8,128)}) async-done(((f32[64,1024]{1,0:T(8,128)}, f32[64,1024]{1,0:T(8,128)}), (f32[64,1024]{1,0:T(8,128)}, f32[64,1024]{1,0:T(8,128)})) %all-reduce.25.cloned.1.call-update) | async-done | bytes 524304 | tf_op jit(solution)/shard_map/psum | solution.py:9
  666.3 12.9 %convolution_subtract_fusion.1 = f32[2048,1024]{1,0:T(8,128)S(1)} fusion(f32[2048,1024]{1,0:T(8,128)} %copy-done, f32[64,2048]{1,0:T(8,128)S(1)} %fusion.1, f32[64,2048]{1,0:T(8,128)S(1)} %bitcast.88, f32[64,1024]{1,0:T(8,128)S(1)} %copy-done.3, f32[64,1024]{1,0:T(8,128)} %get-tuple-element.5), kind=kOutput, calls=%fused_computation.1 | convolution fusion | flops 3223715840 | bytes 18350080 | tf_op jit(solution)/shard_map/dot_general | solution.py:56
  679.2 3.4 copy-done.2
  682.6 8.9 %fusion.68 = f32[64,2048]{1,0:T(8,128)} fusion(f32[64,1024]{1,0:T(8,128)S(1)} %copy-done.5, f32[2048,1024]{1,0:T(8,128)S(1)} %convolution_subtract_fusion.1), kind=kOutput, calls=%fused_computation.88 | convolution fusion | flops 1610612736 | bytes 9175040 | tf_op jit(solution)/shard_map/dot_general | solution.py:28
  691.6 84.2 %all-reduce.21.cloned.1.call-done = f32[64,2048]{1,0:T(8,128)} async-done(((f32[64,2048]{1,0:T(8,128)}), f32[64,2048]{1,0:T(8,128)}) %all-reduce.21.cloned.1.call-update) | async-done | bytes 524304 | tf_op jit(solution)/shard_map/psum | solution.py:35
  775.8 1.7 fusion.30
  778.1 24.8 %psum.126 = f32[64,64]{0,1:T(8,128)S(1)} all-reduce(f32[64,64]{0,1:T(8,128)S(1)} %convolution_bitcast_fusion), channel_id=1, replica_groups=mesh['row'=8,'col'=16] {'row'}, use_global_device_ids=true, to_apply=%region_14.15 | all-reduce | flops 4096 | bytes 32768 | tf_op jit(solution)/shard_map/psum | solution.py:46
  803.0 0.6 fusion
  803.6 0.7 dynamic-slice_select_fusion
  804.3 56.4 %all-reduce.23.cloned.1.call-done = f32[64,1024]{1,0:T(8,128)} async-done(((f32[64,1024]{1,0:T(8,128)}), f32[64,1024]{1,0:T(8,128)}) %all-reduce.23.cloned.1.call-update) | async-done | bytes 262160 | tf_op jit(solution)/shard_map/psum | solution.py:9
  860.7 11.2 %convolution_subtract_fusion = f32[2048,1024]{1,0:T(8,128)} fusion(f32[2048,1024]{1,0:T(8,128)} %copy-done.2, f32[64,2048]{1,0:T(8,128)S(1)} %fusion, f32[64,2048]{1,0:T(8,128)S(1)} %bitcast.90, f32[64,1024]{1,0:T(8,128)S(1)} %copy-done.5, f32[64,1024]{1,0:T(8,128)} %all-reduce.23.cloned.1.call-done), kind=kOutput, calls=%fused_computation | convolution fusion | flops 3223715840 | bytes 18350080 | tf_op jit(solution)/shard_map/dot_general | solution.py:56
  (36 shorter events, 2.5 us)
Async XLA Ops:
  6.5 183.3 %copy-start.7 = (f32[4,64,64]{2,1,0:T(8,128)S(1)}, f32[4,64,64]{2,1,0:T(8,128)}, u32[]{:S(2)}) copy-start(f32[4,64,64]{2,1,0:T(8,128)} %param.5) | copy-start | bytes 196612
  6.5 86.9 %all-reduce.13.cloned.1.call-start = ((), (), s32[]{:S(2)}) async-start(), calls=%async_computation | async-start | bytes 524288 | tf_op jit(solution)/shard_map/psum | solution.py:9
  33.4 156.5 %all-reduce.15.cloned.1.call-start = ((), (), s32[]{:S(2)}) async-start(), calls=%async_computation.1 | async-start | bytes 1048576 | tf_op jit(solution)/shard_map/psum | solution.py:35
  93.4 182.2 %copy-start.6 = (f32[64,1024]{1,0:T(8,128)S(1)}, f32[64,1024]{1,0:T(8,128)}, u32[]{:S(2)}) copy-start(f32[64,1024]{1,0:T(8,128)} %all-reduce.13.cloned.1.call-done) | copy-start | bytes 786436
  105.7 169.9 %all-reduce.29.cloned.1.call-start = ((), (), s32[]{:S(2)}) async-start(), calls=%async_computation.8 | async-start | bytes 1048576 | tf_op jit(solution)/shard_map/psum | solution.py:9
  218.1 167.2 %all-reduce.17.cloned.1.call-start = ((), (), s32[]{:S(2)}) async-start(), calls=%async_computation.2 | async-start | bytes 1048576 | tf_op jit(solution)/shard_map/psum | solution.py:35
  275.6 16.3 %copy-start.4 = (f32[64,1024]{1,0:T(8,128)S(1)}, f32[64,1024]{1,0:T(8,128)}, u32[]{:S(2)}) copy-start(f32[64,1024]{1,0:T(8,128)} %get-tuple-element.10) | copy-start | bytes 786436
  288.4 3.4 copy-start.1
  300.8 170.2 %all-reduce.27.cloned.1.call-start = ((), (), s32[]{:S(2)}) async-start(), calls=%async_computation.7 | async-start | bytes 1048576 | tf_op jit(solution)/shard_map/psum | solution.py:9
  413.4 167.3 %all-reduce.19.cloned.1.call-start = ((), (), s32[]{:S(2)}) async-start(), calls=%async_computation.3 | async-start | bytes 1048576 | tf_op jit(solution)/shard_map/psum | solution.py:35
  471.0 16.3 %copy-start.3 = (f32[64,1024]{1,0:T(8,128)S(1)}, f32[64,1024]{1,0:T(8,128)}, u32[]{:S(2)}) copy-start(f32[64,1024]{1,0:T(8,128)} %get-tuple-element.8) | copy-start | bytes 786436
  483.9 3.4 copy-start
  496.2 170.1 %all-reduce.25.cloned.1.call-start = ((), (), s32[]{:S(2)}) async-start(), calls=%async_computation.6 | async-start | bytes 1048576 | tf_op jit(solution)/shard_map/psum | solution.py:9
  608.8 167.0 %all-reduce.21.cloned.1.call-start = ((), (), s32[]{:S(2)}) async-start(), calls=%async_computation.4 | async-start | bytes 1048576 | tf_op jit(solution)/shard_map/psum | solution.py:35
  666.3 16.3 %copy-start.5 = (f32[64,1024]{1,0:T(8,128)S(1)}, f32[64,1024]{1,0:T(8,128)}, u32[]{:S(2)}) copy-start(f32[64,1024]{1,0:T(8,128)} %get-tuple-element.6) | copy-start | bytes 786436
  679.2 3.4 copy-start.2
  691.5 169.2 %all-reduce.23.cloned.1.call-start = ((), (), s32[]{:S(2)}) async-start(), calls=%async_computation.5 | async-start | bytes 524288 | tf_op jit(solution)/shard_map/psum | solution.py:9
Sparse Core Ops, SparseCore 0:
  33.5 59.8 all-reduce.12
  105.8 84.0 all-reduce.14
  218.2 57.3 all-reduce.28
  300.9 84.2 all-reduce.16
  413.5 57.4 all-reduce.26
  496.3 84.2 all-reduce.18
  608.9 57.3 all-reduce.24
  691.6 84.1 all-reduce.20
  804.4 56.2 all-reduce.22
where the time goes:
time: 886 us; the launch traced here: 879 us
  waiting for transfers between devices  547 us (62%)
  blocking collectives  199 us (22%)
  matrix products  101 us (11%)
  between operations  13.6 us (2%)
  local copies, waits for them, and re-layouts  11 us (1%)
    psum x5, waiting for transfers between devices, broadcast(): return lax.psum(kept, axis)  288 us
    psum x4, waiting for transfers between devices, shards(): product_rows = lax.psum(partial_value, 'col')  259 us
    all_gather x4, blocking collectives, shards(): reflect_rows = lax.all_gather(piece, 'col', axis=1, tiled=True)  101 us
    psum x4, blocking collectives, shards(): inner = lax.psum(local_inner, 'row')  98.1 us
    dot_general x4, matrix products, shards(): lax.dot_general(left_block, right_block, (((0,), (0,)), ((), ())), precis...  49.8 us
    dot_general x4, matrix products, shards(): lax.dot_general(reflect_cols, matrix, (((1,), (1,)), ((), ())), precision...  39 us
  transfers between devices with their start and end apart: 9, of which 9 were waited for; matrix products, arithmetic and copies ran while one was open for 0% of the time, Pallas kernels for 0%

commit v1 on v0

--- a/solution.py
+++ b/solution.py
@@ -32,7 +32,11 @@
             precision=highest,
             preferred_element_type=jnp.float32,
         )
-        product_rows = lax.psum(partial_value, "col")
+        product_rows = partial_value
+        for hop in (1, 2, 4, 8):
+            product_rows = product_rows + lax.ppermute(
+                product_rows, "col", [(dev, dev ^ hop) for dev in range(16)]
+            )
         image_rows = jnp.dot(
             factor.T, product_rows, precision=highest, preferred_element_type=jnp.float32
         )

time: 886 us -> 817 us (0.922)
  waiting for transfers between devices: 547 us -> 422 us
  starting transfers between devices: 1.09 us -> 39.6 us
  blocking collectives: 199 us -> 225 us
    psum x4 -> x0, waiting for transfers between devices: 259 us -> none  [shards(): product_rows = lax.psum(partial_value, 'col')]
    ppermute x0 -> x16, waiting for transfers between devices: none -> 129 us  [shards(): lax.ppermute(product_rows, 'col', [(dev, dev ^ hop) for dev in range(16)])]
    ppermute x0 -> x16, starting transfers between devices: none -> 39.3 us  [shards(): lax.ppermute(product_rows, 'col', [(dev, dev ^ hop) for dev in range(16)])]
    psum x4, blocking collectives: 98.1 us -> 118 us  [shards(): inner = lax.psum(local_inner, 'row')]
  transfers between devices with their start and end apart: 9 -> 21, of which waited for: 9 -> 18; matrix products, arithmetic and copies ran while one was open for 0% -> 0% of each run, Pallas kernels for 0% -> 0%
where the time goes in v1:
time: 817 us; the launch traced here: 811 us
  waiting for transfers between devices  422 us (52%)
  blocking collectives  225 us (28%)
  matrix products  93.3 us (11%)
  starting transfers between devices  39.6 us (5%)
  between operations  13.6 us (2%)
  local copies, waits for them, and re-layouts  11 us (1%)
    psum x5, waiting for transfers between devices, broadcast(): return lax.psum(kept, axis)  293 us
    ppermute x16, waiting for transfers between devices, shards(): lax.ppermute(product_rows, 'col', [(dev, dev ^ hop) for dev in range(16)])  129 us
    psum x4, blocking collectives, shards(): inner = lax.psum(local_inner, 'row')  118 us
    all_gather x4, blocking collectives, shards(): reflect_rows = lax.all_gather(piece, 'col', axis=1, tiled=True)  107 us
    dot_general x4, matrix products, shards(): lax.dot_general(left_block, right_block, (((0,), (0,)), ((), ())), precis...  49.8 us
    ppermute x16, starting transfers between devices, shards(): lax.ppermute(product_rows, 'col', [(dev, dev ^ hop) for dev in range(16)])  39.3 us
    dot_general x4, matrix products, shards(): lax.dot_general(reflect_cols, matrix, (((1,), (1,)), ((), ())), precision...  35.7 us
  transfers between devices with their start and end apart: 21, of which 18 were waited for; matrix products, arithmetic and copies ran while one was open for 0% of the time, Pallas kernels for 0%

profile of v1, /device:TPU:0, one launch (start us, length us, event | category | flops | bytes accessed | tf_op | source)
XLA Modules:
  0.0 811.3 jit_solution(6296724533998869244)
XLA Ops:
  7.4 25.2 %all-gather = f32[1,64,2048]{2,1,0:T(8,128)S(1)} all-gather(f32[1,64,128]{2,1,0:T(8,128)S(1)} %get-tuple-element.13), channel_id=2, replica_groups=mesh['row'=8,'col'=16] {'col'}, dimensions={2}, use_global_device_ids=true | all-gather | bytes 557056 | tf_op jit(solution)/shard_map/all_gather | solution.py:24
  33.4 60.0 %all-reduce.9.cloned.1.call-done = f32[64,1024]{1,0:T(8,128)} async-done(((f32[64,1024]{1,0:T(8,128)}), f32[64,1024]{1,0:T(8,128)}) %all-reduce.9.cloned.1.call-update) | async-done | bytes 262160 | tf_op jit(solution)/shard_map/psum | solution.py:9
  93.4 11.4 %fusion.65 = f32[64,2048]{1,0:T(8,128)S(1)} fusion(f32[64,1024]{1,0:T(8,128)} %all-reduce.9.cloned.1.call-done, f32[2048,1024]{1,0:T(8,128)} %param.3), kind=kOutput, calls=%fused_computation.89 | convolution fusion | flops 1610612736 | bytes 9175040 | tf_op jit(solution)/shard_map/dot_general | solution.py:28
  106.4 10.1 %collective-permute-done = f32[64,2048]{1,0:T(8,128)S(1)} collective-permute-done((f32[64,2048]{1,0:T(8,128)S(1)}, f32[64,2048]{1,0:T(8,128)S(1)}, u32[]{:S(2)}, u32[]{:S(2)}) %collective-permute-start) | collective-permute-done | bytes 524320 | tf_op jit(solution)/shard_map/ppermute | solution.py:37
  116.5 3.1 collective-permute-start.1
  119.6 10.2 %collective-permute-done.1 = f32[64,2048]{1,0:T(8,128)S(1)} collective-permute-done((f32[64,2048]{1,0:T(8,128)S(1)}, f32[64,2048]{1,0:T(8,128)S(1)}, u32[]{:S(2)}, u32[]{:S(2)}) %collective-permute-start.1) | collective-permute-done | bytes 524320 | tf_op jit(solution)/shard_map/ppermute | solution.py:37
  129.9 1.6 collective-permute-start.2
  131.5 9.3 %collective-permute-done.2 = f32[64,2048]{1,0:T(8,128)S(1)} collective-permute-done((f32[64,2048]{1,0:T(8,128)S(1)}, f32[64,2048]{1,0:T(8,128)S(1)}, u32[]{:S(2)}, u32[]{:S(2)}) %collective-permute-start.2) | collective-permute-done | bytes 524320 | tf_op jit(solution)/shard_map/ppermute | solution.py:37
  140.9 3.6 collective-permute-start.3
  144.5 27.4 %all-gather.1 = f32[1,64,2048]{2,1,0:T(8,128)S(1)} all-gather(f32[1,64,128]{2,1,0:T(8,128)S(1)} %get-tuple-element.12), channel_id=3, replica_groups=mesh['row'=8,'col'=16] {'col'}, dimensions={2}, use_global_device_ids=true | all-gather | bytes 557056 | tf_op jit(solution)/shard_map/all_gather | solution.py:24
  173.8 29.2 %psum.85 = f32[64,64]{0,1:T(8,128)S(1)} all-reduce(f32[64,64]{0,1:T(8,128)S(1)} %convolution_bitcast_fusion.3), channel_id=1, replica_groups=mesh['row'=8,'col'=16] {'row'}, use_global_device_ids=true, to_apply=%region_1.2 | all-reduce | flops 4096 | bytes 32768 | tf_op jit(solution)/shard_map/psum | solution.py:50
  204.8 58.1 %all-reduce.17.cloned.1.call-done = (f32[64,1024]{1,0:T(8,128)}, f32[64,1024]{1,0:T(8,128)}) async-done(((f32[64,1024]{1,0:T(8,128)}, f32[64,1024]{1,0:T(8,128)}), (f32[64,1024]{1,0:T(8,128)}, f32[64,1024]{1,0:T(8,128)})) %all-reduce.17.cloned.1.call-update) | async-done | bytes 524304 | tf_op jit(solution)/shard_map/psum | solution.py:9
  262.8 12.9 %convolution_subtract_fusion.3 = f32[2048,1024]{1,0:T(8,128)S(1)} fusion(f32[2048,1024]{1,0:T(8,128)} %param.3, f32[64,2048]{1,0:T(8,128)S(1)} %bitcast_subtract_fusion.3, f32[64,2048]{1,0:T(8,128)S(1)} %bitcast.87, f32[64,1024]{1,0:T(8,128)S(1)} %copy-done.6, f32[64,1024]{1,0:T(8,128)} %get-tuple-element.9), kind=kOutput, calls=%fused_computation.3 | convolution fusion | flops 3223715840 | bytes 18350080 | tf_op jit(solution)/shard_map/dot_general | solution.py:60
  275.7 3.4 copy-done.1
  279.1 8.1 fusion.66
  288.8 10.2 %collective-permute-done.4 = f32[64,2048]{1,0:T(8,128)S(1)} collective-permute-done((f32[64,2048]{1,0:T(8,128)S(1)}, f32[64,2048]{1,0:T(8,128)S(1)}, u32[]{:S(2)}, u32[]{:S(2)}) %collective-permute-start.4) | collective-permute-done | bytes 524320 | tf_op jit(solution)/shard_map/ppermute | solution.py:37
  299.1 3.1 collective-permute-start.5
  302.1 10.2 %collective-permute-done.5 = f32[64,2048]{1,0:T(8,128)S(1)} collective-permute-done((f32[64,2048]{1,0:T(8,128)S(1)}, f32[64,2048]{1,0:T(8,128)S(1)}, u32[]{:S(2)}, u32[]{:S(2)}) %collective-permute-start.5) | collective-permute-done | bytes 524320 | tf_op jit(solution)/shard_map/ppermute | solution.py:37
  312.4 1.6 collective-permute-start.6
  314.0 9.3 %collective-permute-done.6 = f32[64,2048]{1,0:T(8,128)S(1)} collective-permute-done((f32[64,2048]{1,0:T(8,128)S(1)}, f32[64,2048]{1,0:T(8,128)S(1)}, u32[]{:S(2)}, u32[]{:S(2)}) %collective-permute-start.6) | collective-permute-done | bytes 524320 | tf_op jit(solution)/shard_map/ppermute | solution.py:37
  323.4 3.6 collective-permute-start.7
  327.0 27.4 %all-gather.2 = f32[1,64,2048]{2,1,0:T(8,128)S(1)} all-gather(f32[1,64,128]{2,1,0:T(8,128)S(1)} %get-tuple-element.14), channel_id=4, replica_groups=mesh['row'=8,'col'=16] {'col'}, dimensions={2}, use_global_device_ids=true | all-gather | bytes 557056 | tf_op jit(solution)/shard_map/all_gather | solution.py:24
  356.3 29.8 %psum.88 = f32[64,64]{0,1:T(8,128)S(1)} all-reduce(f32[64,64]{0,1:T(8,128)S(1)} %convolution_bitcast_fusion.2), channel_id=1, replica_groups=mesh['row'=8,'col'=16] {'row'}, use_global_device_ids=true, to_apply=%region_4.5 | all-reduce | flops 4096 | bytes 32768 | tf_op jit(solution)/shard_map/psum | solution.py:50
  387.6 58.2 %all-reduce.15.cloned.1.call-done = (f32[64,1024]{1,0:T(8,128)}, f32[64,1024]{1,0:T(8,128)}) async-done(((f32[64,1024]{1,0:T(8,128)}, f32[64,1024]{1,0:T(8,128)}), (f32[64,1024]{1,0:T(8,128)}, f32[64,1024]{1,0:T(8,128)})) %all-reduce.15.cloned.1.call-update) | async-done | bytes 524304 | tf_op jit(solution)/shard_map/psum | solution.py:9
  445.8 12.9 %convolution_subtract_fusion.2 = f32[2048,1024]{1,0:T(8,128)S(1)} fusion(f32[2048,1024]{1,0:T(8,128)} %copy-done.1, f32[64,2048]{1,0:T(8,128)S(1)} %bitcast_subtract_fusion.2, f32[64,2048]{1,0:T(8,128)S(1)} %bitcast.85, f32[64,1024]{1,0:T(8,128)S(1)} %copy-done.4, f32[64,1024]{1,0:T(8,128)} %get-tuple-element.7), kind=kOutput, calls=%fused_computation.2 | convolution fusion | flops 3223715840 | bytes 18350080 | tf_op jit(solution)/shard_map/dot_general | solution.py:60
  458.7 3.4 copy-done
  462.1 8.1 fusion.67
  471.8 10.2 %collective-permute-done.8 = f32[64,2048]{1,0:T(8,128)S(1)} collective-permute-done((f32[64,2048]{1,0:T(8,128)S(1)}, f32[64,2048]{1,0:T(8,128)S(1)}, u32[]{:S(2)}, u32[]{:S(2)}) %collective-permute-start.8) | collective-permute-done | bytes 524320 | tf_op jit(solution)/shard_map/ppermute | solution.py:37
  482.1 3.1 collective-permute-start.9
  485.1 10.2 %collective-permute-done.9 = f32[64,2048]{1,0:T(8,128)S(1)} collective-permute-done((f32[64,2048]{1,0:T(8,128)S(1)}, f32[64,2048]{1,0:T(8,128)S(1)}, u32[]{:S(2)}, u32[]{:S(2)}) %collective-permute-start.9) | collective-permute-done | bytes 524320 | tf_op jit(solution)/shard_map/ppermute | solution.py:37
  495.5 1.6 collective-permute-start.10
  497.0 9.3 %collective-permute-done.10 = f32[64,2048]{1,0:T(8,128)S(1)} collective-permute-done((f32[64,2048]{1,0:T(8,128)S(1)}, f32[64,2048]{1,0:T(8,128)S(1)}, u32[]{:S(2)}, u32[]{:S(2)}) %collective-permute-start.10) | collective-permute-done | bytes 524320 | tf_op jit(solution)/shard_map/ppermute | solution.py:37
  506.4 3.6 collective-permute-start.11
  510.1 27.4 %all-gather.3 = f32[1,64,2048]{2,1,0:T(8,128)S(1)} all-gather(f32[1,64,128]{2,1,0:T(8,128)S(1)} %get-tuple-element.11), channel_id=5, replica_groups=mesh['row'=8,'col'=16] {'col'}, dimensions={2}, use_global_device_ids=true | all-gather | bytes 557056 | tf_op jit(solution)/shard_map/all_gather | solution.py:24
  539.3 29.8 %psum.91 = f32[64,64]{0,1:T(8,128)S(1)} all-reduce(f32[64,64]{0,1:T(8,128)S(1)} %convolution_bitcast_fusion.1), channel_id=1, replica_groups=mesh['row'=8,'col'=16] {'row'}, use_global_device_ids=true, to_apply=%region_7.8 | all-reduce | flops 4096 | bytes 32768 | tf_op jit(solution)/shard_map/psum | solution.py:50
  570.7 58.2 %all-reduce.13.cloned.1.call-done = (f32[64,1024]{1,0:T(8,128)}, f32[64,1024]{1,0:T(8,128)}) async-done(((f32[64,1024]{1,0:T(8,128)}, f32[64,1024]{1,0:T(8,128)}), (f32[64,1024]{1,0:T(8,128)}, f32[64,1024]{1,0:T(8,128)})) %all-reduce.13.cloned.1.call-update) | async-done | bytes 524304 | tf_op jit(solution)/shard_map/psum | solution.py:9
  628.9 12.9 %convolution_subtract_fusion.1 = f32[2048,1024]{1,0:T(8,128)S(1)} fusion(f32[2048,1024]{1,0:T(8,128)} %copy-done, f32[64,2048]{1,0:T(8,128)S(1)} %bitcast_subtract_fusion.1, f32[64,2048]{1,0:T(8,128)S(1)} %bitcast.84, f32[64,1024]{1,0:T(8,128)S(1)} %copy-done.3, f32[64,1024]{1,0:T(8,128)} %get-tuple-element.5), kind=kOutput, calls=%fused_computation.1 | convolution fusion | flops 3223715840 | bytes 18350080 | tf_op jit(solution)/shard_map/dot_general | solution.py:60
  641.8 3.4 copy-done.2
  645.2 8.1 fusion.68
  654.8 10.2 %collective-permute-done.12 = f32[64,2048]{1,0:T(8,128)S(1)} collective-permute-done((f32[64,2048]{1,0:T(8,128)S(1)}, f32[64,2048]{1,0:T(8,128)S(1)}, u32[]{:S(2)}, u32[]{:S(2)}) %collective-permute-start.12) | collective-permute-done | bytes 524320 | tf_op jit(solution)/shard_map/ppermute | solution.py:37
  665.1 3.1 collective-permute-start.13
  668.2 10.2 %collective-permute-done.13 = f32[64,2048]{1,0:T(8,128)S(1)} collective-permute-done((f32[64,2048]{1,0:T(8,128)S(1)}, f32[64,2048]{1,0:T(8,128)S(1)}, u32[]{:S(2)}, u32[]{:S(2)}) %collective-permute-start.13) | collective-permute-done | bytes 524320 | tf_op jit(solution)/shard_map/ppermute | solution.py:37
  680.1 9.3 %collective-permute-done.14 = f32[64,2048]{1,0:T(8,128)S(1)} collective-permute-done((f32[64,2048]{1,0:T(8,128)S(1)}, f32[64,2048]{1,0:T(8,128)S(1)}, u32[]{:S(2)}, u32[]{:S(2)}) %collective-permute-start.14) | collective-permute-done | bytes 524320 | tf_op jit(solution)/shard_map/ppermute | solution.py:37
  689.4 3.6 collective-permute-start.15
  693.1 9.7 %collective-permute-done.15 = f32[64,2048]{1,0:T(8,128)S(1)} collective-permute-done((f32[64,2048]{1,0:T(8,128)S(1)}, f32[64,2048]{1,0:T(8,128)S(1)}, u32[]{:S(2)}, u32[]{:S(2)}) %collective-permute-start.15) | collective-permute-done | bytes 524320 | tf_op jit(solution)/shard_map/ppermute | solution.py:37
  704.0 29.0 %psum.94 = f32[64,64]{0,1:T(8,128)S(1)} all-reduce(f32[64,64]{0,1:T(8,128)S(1)} %convolution_bitcast_fusion), channel_id=1, replica_groups=mesh['row'=8,'col'=16] {'row'}, use_global_device_ids=true, to_apply=%region_10.11 | all-reduce | flops 4096 | bytes 32768 | tf_op jit(solution)/shard_map/psum | solution.py:50
  734.5 58.9 %all-reduce.11.cloned.1.call-done = f32[64,1024]{1,0:T(8,128)} async-done(((f32[64,1024]{1,0:T(8,128)}), f32[64,1024]{1,0:T(8,128)}) %all-reduce.11.cloned.1.call-update) | async-done | bytes 262160 | tf_op jit(solution)/shard_map/psum | solution.py:9
  793.4 11.2 %convolution_subtract_fusion = f32[2048,1024]{1,0:T(8,128)} fusion(f32[2048,1024]{1,0:T(8,128)} %copy-done.2, f32[64,2048]{1,0:T(8,128)S(1)} %bitcast_subtract_fusion, f32[64,2048]{1,0:T(8,128)S(1)} %bitcast.86, f32[64,1024]{1,0:T(8,128)S(1)} %copy-done.5, f32[64,1024]{1,0:T(8,128)} %all-reduce.11.cloned.1.call-done), kind=kOutput, calls=%fused_computation | convolution fusion | flops 3223715840 | bytes 18350080 | tf_op jit(solution)/shard_map/dot_general | solution.py:60
  (68 shorter events, 23.3 us)
Async XLA Ops:
  6.5 166.1 %copy-start.7 = (f32[4,64,64]{2,1,0:T(8,128)S(1)}, f32[4,64,64]{2,1,0:T(8,128)}, u32[]{:S(2)}) copy-start(f32[4,64,64]{2,1,0:T(8,128)} %param.5) | copy-start | bytes 196612
  6.5 86.9 %all-reduce.9.cloned.1.call-start = ((), (), s32[]{:S(2)}) async-start(), calls=%async_computation | async-start | bytes 524288 | tf_op jit(solution)/shard_map/psum | solution.py:9
  33.4 229.5 %all-reduce.17.cloned.1.call-start = ((), (), s32[]{:S(2)}) async-start(), calls=%async_computation.4 | async-start | bytes 1048576 | tf_op jit(solution)/shard_map/psum | solution.py:9
  93.4 169.4 %copy-start.6 = (f32[64,1024]{1,0:T(8,128)S(1)}, f32[64,1024]{1,0:T(8,128)}, u32[]{:S(2)}) copy-start(f32[64,1024]{1,0:T(8,128)} %all-reduce.9.cloned.1.call-done) | copy-start | bytes 786436
  104.8 11.7 %collective-permute-start = (f32[64,2048]{1,0:T(8,128)S(1)}, f32[64,2048]{1,0:T(8,128)S(1)}, u32[]{:S(2)}, u32[]{:S(2)}) collective-permute-start(f32[64,2048]{1,0:T(8,128)S(1)} %fusion.65), channel_id=1, source_target_pairs={{0,1},{1,0},{2,3},{3,2},{4,5},{5,4},{6,7},{7,6},{8,9},{9,8},{10,11... | collective-permute-start | bytes 1572872 | tf_op jit(solution)/shard_map/ppermute | solution.py:37
  116.5 13.3 %collective-permute-start.1 = (f32[64,2048]{1,0:T(8,128)S(1)}, f32[64,2048]{1,0:T(8,128)S(1)}, u32[]{:S(2)}, u32[]{:S(2)}) collective-permute-start(f32[64,2048]{1,0:T(8,128)S(1)} %add.89), channel_id=1, source_target_pairs={{0,2},{1,3},{2,0},{3,1},{4,6},{5,7},{6,4},{7,5},{8,10},{9,11},{10,... | collective-permute-start | bytes 1572872 | tf_op jit(solution)/shard_map/ppermute | solution.py:37
  129.9 10.9 %collective-permute-start.2 = (f32[64,2048]{1,0:T(8,128)S(1)}, f32[64,2048]{1,0:T(8,128)S(1)}, u32[]{:S(2)}, u32[]{:S(2)}) collective-permute-start(f32[64,2048]{1,0:T(8,128)S(1)} %add.90), channel_id=1, source_target_pairs={{0,4},{1,5},{2,6},{3,7},{4,0},{5,1},{6,2},{7,3},{8,12},{9,13},{10,... | collective-permute-start | bytes 1572872 | tf_op jit(solution)/shard_map/ppermute | solution.py:37
  140.9 31.8 %collective-permute-start.3 = (f32[64,2048]{1,0:T(8,128)S(1)}, f32[64,2048]{1,0:T(8,128)S(1)}, u32[]{:S(2)}, u32[]{:S(2)}) collective-permute-start(f32[64,2048]{1,0:T(8,128)S(1)} %add.91), channel_id=1, source_target_pairs={{0,8},{1,9},{2,10},{3,11},{4,12},{5,13},{6,14},{7,15},{8,0},{9,1},... | collective-permute-start | bytes 1572872 | tf_op jit(solution)/shard_map/ppermute | solution.py:37
  204.5 241.3 %all-reduce.15.cloned.1.call-start = ((), (), s32[]{:S(2)}) async-start(), calls=%async_computation.3 | async-start | bytes 1048576 | tf_op jit(solution)/shard_map/psum | solution.py:9
  262.8 16.3 %copy-start.4 = (f32[64,1024]{1,0:T(8,128)S(1)}, f32[64,1024]{1,0:T(8,128)}, u32[]{:S(2)}) copy-start(f32[64,1024]{1,0:T(8,128)} %get-tuple-element.10) | copy-start | bytes 786436
  275.7 3.4 copy-start.1
  287.2 11.8 %collective-permute-start.4 = (f32[64,2048]{1,0:T(8,128)S(1)}, f32[64,2048]{1,0:T(8,128)S(1)}, u32[]{:S(2)}, u32[]{:S(2)}) collective-permute-start(f32[64,2048]{1,0:T(8,128)S(1)} %fusion.66), channel_id=1, source_target_pairs={{0,1},{1,0},{2,3},{3,2},{4,5},{5,4},{6,7},{7,6},{8,9},{9,8},{10,11... | collective-permute-start | bytes 1572872 | tf_op jit(solution)/shard_map/ppermute | solution.py:37
  299.1 13.3 %collective-permute-start.5 = (f32[64,2048]{1,0:T(8,128)S(1)}, f32[64,2048]{1,0:T(8,128)S(1)}, u32[]{:S(2)}, u32[]{:S(2)}) collective-permute-start(f32[64,2048]{1,0:T(8,128)S(1)} %add.93), channel_id=1, source_target_pairs={{0,2},{1,3},{2,0},{3,1},{4,6},{5,7},{6,4},{7,5},{8,10},{9,11},{10,... | collective-permute-start | bytes 1572872 | tf_op jit(solution)/shard_map/ppermute | solution.py:37
  312.4 10.9 %collective-permute-start.6 = (f32[64,2048]{1,0:T(8,128)S(1)}, f32[64,2048]{1,0:T(8,128)S(1)}, u32[]{:S(2)}, u32[]{:S(2)}) collective-permute-start(f32[64,2048]{1,0:T(8,128)S(1)} %add.94), channel_id=1, source_target_pairs={{0,4},{1,5},{2,6},{3,7},{4,0},{5,1},{6,2},{7,3},{8,12},{9,13},{10,... | collective-permute-start | bytes 1572872 | tf_op jit(solution)/shard_map/ppermute | solution.py:37
  323.4 31.7 %collective-permute-start.7 = (f32[64,2048]{1,0:T(8,128)S(1)}, f32[64,2048]{1,0:T(8,128)S(1)}, u32[]{:S(2)}, u32[]{:S(2)}) collective-permute-start(f32[64,2048]{1,0:T(8,128)S(1)} %add.95), channel_id=1, source_target_pairs={{0,8},{1,9},{2,10},{3,11},{4,12},{5,13},{6,14},{7,15},{8,0},{9,1},... | collective-permute-start | bytes 1572872 | tf_op jit(solution)/shard_map/ppermute | solution.py:37
  387.6 241.3 %all-reduce.13.cloned.1.call-start = ((), (), s32[]{:S(2)}) async-start(), calls=%async_computation.2 | async-start | bytes 1048576 | tf_op jit(solution)/shard_map/psum | solution.py:9
  445.8 16.3 %copy-start.3 = (f32[64,1024]{1,0:T(8,128)S(1)}, f32[64,1024]{1,0:T(8,128)}, u32[]{:S(2)}) copy-start(f32[64,1024]{1,0:T(8,128)} %get-tuple-element.8) | copy-start | bytes 786436
  458.7 3.4 copy-start
  470.2 11.8 %collective-permute-start.8 = (f32[64,2048]{1,0:T(8,128)S(1)}, f32[64,2048]{1,0:T(8,128)S(1)}, u32[]{:S(2)}, u32[]{:S(2)}) collective-permute-start(f32[64,2048]{1,0:T(8,128)S(1)} %fusion.67), channel_id=1, source_target_pairs={{0,1},{1,0},{2,3},{3,2},{4,5},{5,4},{6,7},{7,6},{8,9},{9,8},{10,11... | collective-permute-start | bytes 1572872 | tf_op jit(solution)/shard_map/ppermute | solution.py:37
  482.1 13.3 %collective-permute-start.9 = (f32[64,2048]{1,0:T(8,128)S(1)}, f32[64,2048]{1,0:T(8,128)S(1)}, u32[]{:S(2)}, u32[]{:S(2)}) collective-permute-start(f32[64,2048]{1,0:T(8,128)S(1)} %add.97), channel_id=1, source_target_pairs={{0,2},{1,3},{2,0},{3,1},{4,6},{5,7},{6,4},{7,5},{8,10},{9,11},{10,... | collective-permute-start | bytes 1572872 | tf_op jit(solution)/shard_map/ppermute | solution.py:37
  495.5 10.9 %collective-permute-start.10 = (f32[64,2048]{1,0:T(8,128)S(1)}, f32[64,2048]{1,0:T(8,128)S(1)}, u32[]{:S(2)}, u32[]{:S(2)}) collective-permute-start(f32[64,2048]{1,0:T(8,128)S(1)} %add.98), channel_id=1, source_target_pairs={{0,4},{1,5},{2,6},{3,7},{4,0},{5,1},{6,2},{7,3},{8,12},{9,13},{10,... | collective-permute-start | bytes 1572872 | tf_op jit(solution)/shard_map/ppermute | solution.py:37
  506.4 31.7 %collective-permute-start.11 = (f32[64,2048]{1,0:T(8,128)S(1)}, f32[64,2048]{1,0:T(8,128)S(1)}, u32[]{:S(2)}, u32[]{:S(2)}) collective-permute-start(f32[64,2048]{1,0:T(8,128)S(1)} %add.99), channel_id=1, source_target_pairs={{0,8},{1,9},{2,10},{3,11},{4,12},{5,13},{6,14},{7,15},{8,0},{9,1},... | collective-permute-start | bytes 1572872 | tf_op jit(solution)/shard_map/ppermute | solution.py:37
  570.6 222.7 %all-reduce.11.cloned.1.call-start = ((), (), s32[]{:S(2)}) async-start(), calls=%async_computation.1 | async-start | bytes 524288 | tf_op jit(solution)/shard_map/psum | solution.py:9
  628.9 16.3 %copy-start.5 = (f32[64,1024]{1,0:T(8,128)S(1)}, f32[64,1024]{1,0:T(8,128)}, u32[]{:S(2)}) copy-start(f32[64,1024]{1,0:T(8,128)} %get-tuple-element.6) | copy-start | bytes 786436
  641.8 3.4 copy-start.2
  653.3 11.8 %collective-permute-start.12 = (f32[64,2048]{1,0:T(8,128)S(1)}, f32[64,2048]{1,0:T(8,128)S(1)}, u32[]{:S(2)}, u32[]{:S(2)}) collective-permute-start(f32[64,2048]{1,0:T(8,128)S(1)} %fusion.68), channel_id=1, source_target_pairs={{0,1},{1,0},{2,3},{3,2},{4,5},{5,4},{6,7},{7,6},{8,9},{9,8},{10,11... | collective-permute-start | bytes 1572872 | tf_op jit(solution)/shard_map/ppermute | solution.py:37
  665.1 13.3 %collective-permute-start.13 = (f32[64,2048]{1,0:T(8,128)S(1)}, f32[64,2048]{1,0:T(8,128)S(1)}, u32[]{:S(2)}, u32[]{:S(2)}) collective-permute-start(f32[64,2048]{1,0:T(8,128)S(1)} %add.101), channel_id=1, source_target_pairs={{0,2},{1,3},{2,0},{3,1},{4,6},{5,7},{6,4},{7,5},{8,10},{9,11},{10,... | collective-permute-start | bytes 1572872 | tf_op jit(solution)/shard_map/ppermute | solution.py:37
  678.5 10.9 %collective-permute-start.14 = (f32[64,2048]{1,0:T(8,128)S(1)}, f32[64,2048]{1,0:T(8,128)S(1)}, u32[]{:S(2)}, u32[]{:S(2)}) collective-permute-start(f32[64,2048]{1,0:T(8,128)S(1)} %add.102), channel_id=1, source_target_pairs={{0,4},{1,5},{2,6},{3,7},{4,0},{5,1},{6,2},{7,3},{8,12},{9,13},{10,... | collective-permute-start | bytes 1572872 | tf_op jit(solution)/shard_map/ppermute | solution.py:37
  689.4 13.3 %collective-permute-start.15 = (f32[64,2048]{1,0:T(8,128)S(1)}, f32[64,2048]{1,0:T(8,128)S(1)}, u32[]{:S(2)}, u32[]{:S(2)}) collective-permute-start(f32[64,2048]{1,0:T(8,128)S(1)} %add.103), channel_id=1, source_target_pairs={{0,8},{1,9},{2,10},{3,11},{4,12},{5,13},{6,14},{7,15},{8,0},{9,1},... | collective-permute-start | bytes 1572872 | tf_op jit(solution)/shard_map/ppermute | solution.py:37
Sparse Core Ops, SparseCore 0:
  33.5 59.8 all-reduce.8
  204.7 58.1 all-reduce.16
  387.7 58.0 all-reduce.14
  570.7 58.0 all-reduce.12
  734.6 58.7 all-reduce.10
